TPU v7x, 32 devices: a whole 2x2x4 slice. The times are simulated.
32 devices in a mesh: groups: 2 (over y), rows: 4 (over z), cols: 2 (over x), sub: 2 (over core).
Axes of the slice: x: 2, y: 2, z: 4, core: 2. Of those that a mesh axis runs over, the one named last changes fastest.
Arguments:
- features: bfloat16 [128, 256, 512], P(None, ('groups', 'rows'), ('cols', 'sub')), parts along dimension 1, may hold values from -9 to 9
- guide_image: bfloat16 [3, 256, 512], P(None, ('groups', 'rows'), ('cols', 'sub')), parts along dimension 1, may hold values from 0 to 1
- conv_weight: bfloat16 [3, 3, 64, 128], replicated, may hold values from -0.1875 to 0.1875
- head_weight: float32 [2, 64], replicated, may hold values from -0.75 to 0.75
- pixel_mask: int32 [256, 512], P(('groups', 'rows', 'cols', 'sub')), parts along dimension 0, may hold values 0 or 1
Outputs:
- mixture: float32 [256, 512], P(('groups', 'rows', 'cols', 'sub')), parts along dimension 0
There are 2 independent parts, one for each index of `groups`. A program takes and returns all parts, laid end to end along the dimension named above; an argument that names none is the same for every part. Nothing has to cross between parts.
All inputs are finite; a program needn't handle non-finite values. No bound on the sum of `pixel_mask` on one device may be relied on, other than what follows from the above.
Results may differ from a plain program's by a relative error of at most 0.0003.
Values may be sent and summed in bfloat16 or wider, within the bound.
A program may use at most 64 MiB of HBM per device.

v0:
```python
import jax
import jax.numpy as jnp
from jax import lax
from jax.sharding import PartitionSpec as P

ITERS = 2


RIDGE = 0.05
BASE_WEIGHT = 0.1


def with_halo(cells, sides, width):
    for axis, dim in sides:
        count = lax.axis_size(axis)
        ends = count - 1
        head = lax.slice_in_dim(cells, 0, width, axis=dim)
        tail = lax.slice_in_dim(cells, cells.shape[dim] - width, cells.shape[dim], axis=dim)
        cells = jnp.concatenate(
            [
                lax.ppermute(tail, axis, [(i, (i + 1) % count) for i in range(ends)]),
                cells,
                lax.ppermute(head, axis, [((i + 1) % count, i) for i in range(ends)]),
            ],
            axis=dim,
        )
    return cells


def box_sum(extended):
    vertical = extended[:, :-2, :] + extended[:, 1:-1, :] + extended[:, 2:, :]
    return vertical[:, :, :-2] + vertical[:, :, 1:-1] + vertical[:, :, 2:]


def window_stats(guide_ext):
    average = box_sum(guide_ext) / 9.0
    red_ext, green_ext, blue_ext = (guide_ext[0], guide_ext[1], guide_ext[2])
    products = jnp.stack(
        [
            red_ext * red_ext,
            red_ext * green_ext,
            red_ext * blue_ext,
            green_ext * green_ext,
            green_ext * blue_ext,
            blue_ext * blue_ext,
        ]
    )
    second = box_sum(products) / 9.0
    cov_rr = second[0] - average[0] * average[0] + RIDGE
    cov_rg = second[1] - average[0] * average[1]
    joint_spread_redyellow = second[2] - average[0] * average[2]
    cov_gg = second[3] - average[1] * average[1] + RIDGE
    covariance_green_blue = second[4] - average[1] * average[2]
    cov_bb = second[5] - average[2] * average[2] + RIDGE
    cof_rr = cov_gg * cov_bb - covariance_green_blue * covariance_green_blue
    cof_rg = joint_spread_redyellow * covariance_green_blue - cov_rg * cov_bb
    cof_rb = cov_rg * covariance_green_blue - joint_spread_redyellow * cov_gg
    cof_gg = cov_rr * cov_bb - joint_spread_redyellow * joint_spread_redyellow
    cofactor_green_blue = cov_rg * joint_spread_redyellow - cov_rr * covariance_green_blue
    cof_bb = cov_rr * cov_gg - cov_rg * cov_rg
    determinant = cov_rr * cof_rr + cov_rg * cof_rg + joint_spread_redyellow * cof_rb
    inverse = jnp.stack([cof_rr, cof_rg, cof_rb, cof_gg, cofactor_green_blue, cof_bb]) / determinant
    return (average, inverse)


def coefficients(field_ext, guide_ext, average, inverse):
    field_box = box_sum(field_ext)[0] / 9.0
    crossed = box_sum(guide_ext * field_ext) / 9.0 - average * field_box
    slope_r = inverse[0] * crossed[0] + inverse[1] * crossed[1] + inverse[2] * crossed[2]
    slope_g = inverse[1] * crossed[0] + inverse[3] * crossed[1] + inverse[4] * crossed[2]
    gradient_coefficient_third = (
        inverse[2] * crossed[0] + inverse[4] * crossed[1] + inverse[5] * crossed[2]
    )
    offset = field_box - (
        slope_r * average[0] + slope_g * average[1] + gradient_coefficient_third * average[2]
    )
    return jnp.stack([slope_r, slope_g, gradient_coefficient_third, offset])


def apply_operator(field_map, coef_ext, guide_local_tile, weights):
    summed = box_sum(coef_ext)
    smooth = (
        summed[0] * guide_local_tile[0]
        + summed[1] * guide_local_tile[1]
        + summed[2] * guide_local_tile[2]
        + summed[3]
    )
    return 9.0 * field_map - smooth + weights * field_map


def head_maps(extended, conv_weight, head_weight, height, columns):
    channels = extended.shape[0]
    accumulated = jnp.zeros((conv_weight.shape[2], height * columns), jnp.float32)
    for shift_r in range(3):
        for shift_c in range(3):
            window_cell_count = extended[
                :, shift_r : shift_r + height, shift_c : shift_c + columns
            ].reshape(channels, height * columns)
            accumulated = accumulated + jnp.dot(
                conv_weight[shift_r, shift_c], window_cell_count, preferred_element_type=jnp.float32
            )
    hidden = jnp.maximum(accumulated, 0.0)
    logits = jnp.dot(head_weight, hidden, precision=lax.Precision.HIGHEST)
    seed_map = jax.nn.sigmoid(logits[0])
    certainty = jax.nn.softplus(logits[1])
    return jnp.stack([seed_map, certainty]).reshape(2, height, columns)


def pad_columns(stack):
    return jnp.pad(stack, ((0, 0), (0, 0), (1, 1)))


def strip_rim(stack):
    return pad_columns(with_halo(stack, ((("rows", "cols", "sub"), 1),), 1))


def global_sums(values):
    return lax.psum((values[0], values[1]), ("rows", "cols", "sub"))


def on_device(features, guide_image, conv_weight, head_weight, pixel_mask):
    tile_rows, tile_cols = (features.shape[1], features.shape[2])
    outgoing = (features, guide_image)
    rimmed = (
        with_halo(outgoing[0], (("rows", 1), (("cols", "sub"), 2)), 1),
        with_halo(outgoing[1], (("rows", 1), (("cols", "sub"), 2)), 1),
    )
    predictor_result = head_maps(rimmed[0], conv_weight, head_weight, tile_rows, tile_cols)
    guide_float = guide_image.astype(jnp.float32)
    tile_average, tile_inverse_matrix = window_stats(rimmed[1].astype(jnp.float32))
    stacked = jnp.concatenate([predictor_result, guide_float, tile_average, tile_inverse_matrix])
    strips = lax.all_to_all(stacked, ("cols", "sub"), split_axis=1, concat_axis=2, tiled=True)
    seed_map = strips[0]
    certainty = strips[1]
    guide_local_tile = strips[2:5]
    guide_ext = strip_rim(guide_local_tile)
    average, inverse = (strips[5:8], strips[8:14])
    weights = BASE_WEIGHT + pixel_mask.astype(jnp.float32) * certainty

    def operate(field_map):
        field_ext = strip_rim(field_map[None])
        coef = coefficients(field_ext, guide_ext, average, inverse)
        coef_ext = strip_rim(coef)
        return apply_operator(field_map, coef_ext, guide_local_tile, weights)

    mixture = seed_map
    residual = weights * seed_map - operate(seed_map)
    image_dir = operate(residual)
    norm_now, product = global_sums((jnp.sum(residual * residual), jnp.sum(residual * image_dir)))
    step_size = norm_now / product
    direction, along = (residual, image_dir)
    for iteration in range(ITERS):
        mixture = mixture + step_size * direction
        residual = residual - step_size * along
        if iteration + 1 < ITERS:
            image_dir = operate(residual)
            norm_next, product = global_sums(
                (jnp.sum(residual * residual), jnp.sum(residual * image_dir))
            )
            ratio = norm_next / norm_now
            step_size = norm_next / (product - ratio * norm_next / step_size)
            direction = residual + ratio * direction
            along = image_dir + ratio * along
            norm_now = norm_next
    return mixture


def solution(mesh):
    return jax.shard_map(
        on_device,
        mesh=mesh,
        in_specs=(
            P(None, ("groups", "rows"), ("cols", "sub")),
            P(None, ("groups", "rows"), ("cols", "sub")),
            P(),
            P(),
            P(("groups", "rows", "cols", "sub"), None),
        ),
        out_specs=P(("groups", "rows", "cols", "sub"), None),
        check_vma=False,
    )
```

profile of v0, /device:TPU:0, one launch (start us, length us, event | category | flops | bytes accessed | tf_op | source)
XLA Modules:
  0.0 178.0 jit_solution(652070751891009587)
XLA Ops:
  0.8 4.9 %collective-permute-start.4 = (bf16[3,1,128]{2,1,0:T(2,128)(2,1)S(1)}, bf16[3,1,128]{2,1,0:T(2,128)(2,1)S(1)}, u32[]{:S(2)}, u32[]{:S(2)}) collective-permute-start(bf16[3,1,128]{2,1,0:T(2,128)(2,1)S(1)} %get-tuple-element.77), channel_id=1, source_target_pairs={{0,4},{4,8},{8,12},{1,5},{5,9},{9,13},{2,6},{6,10},{10,14},{3,7},{... | collective-permute-start | bytes 2312 | tf_op jit(solution)/shard_map/ppermute | solution.py:21
  5.7 1.3 collective-permute-start.5
  7.0 2.5 %copy.68 = bf16[128,32,128]{0,1,2:T(8,128)(2,1)S(1)} copy(bf16[128,32,128]{2,1,0:T(8,128)(2,1)} %param.5) | data formatting | bytes 2097152 | tf_op args[0]
  9.6 1.6 collective-permute-done.5
  12.6 1.3 collective-permute-start.7
  13.9 4.1 %collective-permute-start = (bf16[128,1,128]{0,1,2:T(2,128)(2,1)S(1)}, bf16[128,1,128]{0,1,2:T(2,128)(2,1)}, u32[]{:S(2)}, u32[]{:S(2)}) collective-permute-start(bf16[128,1,128]{0,1,2:T(2,128)(2,1)S(1)} %get-tuple-element.47), channel_id=1, source_target_pairs={{0,4},{4,8},{8,12},{1,5},{5,9},{9,13},{2,6},{6,10},{10,14},{3,7},{... | collective-permute-start | bytes 98312 | tf_op jit(solution)/shard_map/ppermute | solution.py:21
  19.7 4.5 %collective-permute-done.1 = bf16[128,1,128]{0,1,2:T(2,128)(2,1)} collective-permute-done((bf16[128,1,128]{0,1,2:T(2,128)(2,1)S(1)}, bf16[128,1,128]{0,1,2:T(2,128)(2,1)}, u32[]{:S(2)}, u32[]{:S(2)}) %collective-permute-start.1) | collective-permute-done | bytes 32800 | tf_op jit(solution)/shard_map/ppermute | solution.py:23
  24.2 1.6 pad_maximum_fusion
  26.8 3.9 %collective-permute-start.2 = (bf16[128,34,1]{0,1,2:T(8,128)(2,1)}, bf16[128,34,1]{0,1,2:T(8,128)(2,1)}, u32[]{:S(2)}, u32[]{:S(2)}) collective-permute-start(bf16[128,34,1]{0,1,2:T(8,128)(2,1)} %get-tuple-element.37), channel_id=1, source_target_pairs={{0,1},{1,2},{2,3},{4,5},{5,6},{6,7},{8,9},{9,10},{10,11},{12,13},{... | collective-permute-start | bytes 26120 | tf_op jit(solution)/shard_map/ppermute | solution.py:21
  32.0 1.6 copy.73
  33.6 1.6 copy.76
  35.2 2.1 %pad_maximum_fusion.3 = (bf16[128,32,128]{2,1,0:T(8,128)(2,1)S(1)}, bf16[128,32,128]{2,1,0:T(8,128)(2,1)S(1)}) fusion(bf16[128,32,128]{2,1,0:T(8,128)(2,1)S(1)} %copy-done.1, bf16[128,1,128]{2,1,0:T(2,128)(2,1)} %copy.73, bf16[128,1,128]{2,1,0:T(2,128)(2,1)} %copy.76), kind=kLoop, calls=%fused_computation.30 | loop fusion | flops 4194304 | bytes 3211264 | tf_op jit(solution)/shard_map/concatenate | solution.py:19
  46.4 12.0 %all_to_all.15 = f32[14,32,128]{2,0,1:T(8,128)S(1)} all-to-all(f32[14,32,128]{2,0,1:T(8,128)S(1)} %copy.77), channel_id=1, replica_groups=mesh['groups'=2,'rows'=4,'cols'=2,'sub'=2] {'cols','sub'}, dimensions={1} | all-to-all | bytes 458752 | tf_op jit(solution)/shard_map/all_to_all | solution.py:132
  58.6 1.4 collective-permute-start.10
  60.0 1.3 collective-permute-start.11
  61.3 3.5 %collective-permute-start.8 = (f32[3,1,512]{2,1,0:T(1,128)S(1)}, f32[3,1,512]{2,1,0:T(1,128)S(1)}, u32[]{:S(2)}, u32[]{:S(2)}) collective-permute-start(f32[3,1,512]{2,1,0:T(1,128)S(1)} %get-tuple-element.71), channel_id=1, source_target_pairs={{0,1},{1,2},{2,3},{3,4},{4,5},{5,6},{6,7},{7,8},{8,9},{9,10},{10,1... | collective-permute-start | bytes 18440 | tf_op jit(solution)/shard_map/ppermute | solution.py:21
  64.8 1.3 collective-permute-start.9
  66.4 2.8 %collective-permute-done.9 = f32[3,1,512]{2,1,0:T(1,128)S(1)} collective-permute-done((f32[3,1,512]{2,1,0:T(1,128)S(1)}, f32[3,1,512]{2,1,0:T(1,128)S(1)}, u32[]{:S(2)}, u32[]{:S(2)}) %collective-permute-start.9) | collective-permute-done | bytes 6176 | tf_op jit(solution)/shard_map/ppermute | solution.py:23
  69.5 4.3 %collective-permute-start.12 = (f32[4,1,512]{2,1,0:T(1,128)S(1)}, f32[4,1,512]{2,1,0:T(1,128)S(1)}, u32[]{:S(2)}, u32[]{:S(2)}) collective-permute-start(f32[4,1,512]{2,1,0:T(1,128)S(1)} %get-tuple-element.69), channel_id=1, source_target_pairs={{0,1},{1,2},{2,3},{3,4},{4,5},{5,6},{6,7},{7,8},{8,9},{9,10},{10,1... | collective-permute-start | bytes 24584 | tf_op jit(solution)/shard_map/ppermute | solution.py:21
  73.8 1.3 collective-permute-start.13
  75.1 2.0 %collective-permute-done.13 = f32[4,1,512]{2,1,0:T(1,128)S(1)} collective-permute-done((f32[4,1,512]{2,1,0:T(1,128)S(1)}, f32[4,1,512]{2,1,0:T(1,128)S(1)}, u32[]{:S(2)}, u32[]{:S(2)}) %collective-permute-start.13) | collective-permute-done | bytes 8224 | tf_op jit(solution)/shard_map/ppermute | solution.py:23
  77.4 5.9 %collective-permute-start.14 = (f32[1,1,512]{2,1,0:T(1,128)S(1)}, f32[1,1,512]{2,1,0:T(1,128)S(1)}, u32[]{:S(2)}, u32[]{:S(2)}) collective-permute-start(f32[1,1,512]{2,1,0:T(1,128)S(1)} %get-tuple-element.87), channel_id=1, source_target_pairs={{0,1},{1,2},{2,3},{3,4},{4,5},{5,6},{6,7},{7,8},{8,9},{9,10},{10,1... | collective-permute-start | bytes 6152 | tf_op jit(solution)/shard_map/ppermute | solution.py:21
  83.3 1.3 collective-permute-start.15
  84.6 1.7 collective-permute-done.15
  86.9 4.7 %collective-permute-start.16 = (f32[4,1,512]{2,1,0:T(1,128)S(1)}, f32[4,1,512]{2,1,0:T(1,128)S(1)}, u32[]{:S(2)}, u32[]{:S(2)}) collective-permute-start(f32[4,1,512]{2,1,0:T(1,128)S(1)} %get-tuple-element.67), channel_id=1, source_target_pairs={{0,1},{1,2},{2,3},{3,4},{4,5},{5,6},{6,7},{7,8},{8,9},{9,10},{10,1... | collective-permute-start | bytes 24584 | tf_op jit(solution)/shard_map/ppermute | solution.py:21
  92.9 1.8 collective-permute-done.17
  95.6 33.0 %all-reduce.8 = (f32[]{:T(128)}, f32[]{:T(128)}) all-reduce(f32[]{:T(128)} %get-tuple-element.8, f32[]{:T(128)} %get-tuple-element.7), channel_id=1, replica_groups=mesh['groups'=2,'rows'=4,'cols'=2,'sub'=2] {'rows','cols','sub'}, use_global_device_ids=true, to_apply=%region_1.2 | all-reduce | flops 2 | bytes 16 | tf_op jit(solution)/shard_map/psum | solution.py:118
  132.5 1.7 collective-permute-done.19
  134.8 2.1 %collective-permute-start.20 = (f32[4,1,512]{2,1,0:T(1,128)S(1)}, f32[4,1,512]{2,1,0:T(1,128)S(1)}, u32[]{:S(2)}, u32[]{:S(2)}) collective-permute-start(f32[4,1,512]{2,1,0:T(1,128)S(1)} %get-tuple-element.65), channel_id=1, source_target_pairs={{0,1},{1,2},{2,3},{3,4},{4,5},{5,6},{6,7},{7,8},{8,9},{9,10},{10,1... | collective-permute-start | bytes 24584 | tf_op jit(solution)/shard_map/ppermute | solution.py:21
  136.9 1.3 collective-permute-start.21
  138.2 1.8 collective-permute-done.21
  140.9 32.0 %all-reduce.7 = (f32[]{:T(128)}, f32[]{:T(128)}) all-reduce(f32[]{:T(128)} %get-tuple-element.6, f32[]{:T(128)} %get-tuple-element.5), channel_id=1, replica_groups=mesh['groups'=2,'rows'=4,'cols'=2,'sub'=2] {'rows','cols','sub'}, use_global_device_ids=true, to_apply=%region_5.6 | all-reduce | flops 2 | bytes 16 | tf_op jit(solution)/shard_map/psum | solution.py:118
  (121 shorter events, 23.4 us)
Async XLA Ops:
  0.0 45.1 %copy-start = (f32[2,64]{1,0:T(2,128)S(1)}, f32[2,64]{1,0:T(2,128)}, u32[]{:S(2)}) copy-start(f32[2,64]{1,0:T(2,128)} %param.8) | copy-start | bytes 1540
  0.0 11.2 %copy-start.2 = (bf16[3,32,128]{2,1,0:T(8,128)(2,1)S(1)}, bf16[3,32,128]{2,1,0:T(8,128)(2,1)}, u32[]{:S(2)}) copy-start(bf16[3,32,128]{2,1,0:T(8,128)(2,1)} %param.6) | copy-start | bytes 73732
  0.8 8.8 %collective-permute-start.4 = (bf16[3,1,128]{2,1,0:T(2,128)(2,1)S(1)}, bf16[3,1,128]{2,1,0:T(2,128)(2,1)S(1)}, u32[]{:S(2)}, u32[]{:S(2)}) collective-permute-start(bf16[3,1,128]{2,1,0:T(2,128)(2,1)S(1)} %get-tuple-element.77), channel_id=1, source_target_pairs={{0,4},{4,8},{8,12},{1,5},{5,9},{9,13},{2,6},{6,10},{10,14},{3,7},{... | collective-permute-start | bytes 2312 | tf_op jit(solution)/shard_map/ppermute | solution.py:21
  5.7 5.5 %collective-permute-start.5 = (bf16[3,1,128]{2,1,0:T(2,128)(2,1)S(1)}, bf16[3,1,128]{2,1,0:T(2,128)(2,1)S(1)}, u32[]{:S(2)}, u32[]{:S(2)}) collective-permute-start(bf16[3,1,128]{2,1,0:T(2,128)(2,1)S(1)} %get-tuple-element.78), channel_id=1, source_target_pairs={{4,0},{8,4},{12,8},{5,1},{9,5},{13,9},{6,2},{10,6},{14,10},{7,3},{... | collective-permute-start | bytes 2312 | tf_op jit(solution)/shard_map/ppermute | solution.py:23
  11.3 8.0 %collective-permute-start.6 = (bf16[3,34,1]{2,1,0:T(8,128)(2,1)S(1)}, bf16[3,34,1]{2,1,0:T(8,128)(2,1)S(1)}, u32[]{:S(2)}, u32[]{:S(2)}) collective-permute-start(bf16[3,34,1]{2,1,0:T(8,128)(2,1)S(1)} %get-tuple-element.75), channel_id=1, source_target_pairs={{0,1},{1,2},{2,3},{4,5},{5,6},{6,7},{8,9},{9,10},{10,11},{12,13},{... | collective-permute-start | bytes 620 | tf_op jit(solution)/shard_map/ppermute | solution.py:21
  12.6 6.7 %collective-permute-start.7 = (bf16[3,34,1]{2,1,0:T(8,128)(2,1)S(1)}, bf16[3,34,1]{2,1,0:T(8,128)(2,1)S(1)}, u32[]{:S(2)}, u32[]{:S(2)}) collective-permute-start(bf16[3,34,1]{2,1,0:T(8,128)(2,1)S(1)} %get-tuple-element.76), channel_id=1, source_target_pairs={{1,0},{2,1},{3,2},{5,4},{6,5},{7,6},{9,8},{10,9},{11,10},{13,12},{... | collective-permute-start | bytes 620 | tf_op jit(solution)/shard_map/ppermute | solution.py:23
  13.9 5.8 %collective-permute-start = (bf16[128,1,128]{0,1,2:T(2,128)(2,1)S(1)}, bf16[128,1,128]{0,1,2:T(2,128)(2,1)}, u32[]{:S(2)}, u32[]{:S(2)}) collective-permute-start(bf16[128,1,128]{0,1,2:T(2,128)(2,1)S(1)} %get-tuple-element.47), channel_id=1, source_target_pairs={{0,4},{4,8},{8,12},{1,5},{5,9},{9,13},{2,6},{6,10},{10,14},{3,7},{... | collective-permute-start | bytes 98312 | tf_op jit(solution)/shard_map/ppermute | solution.py:21
  18.0 6.3 %collective-permute-start.1 = (bf16[128,1,128]{0,1,2:T(2,128)(2,1)S(1)}, bf16[128,1,128]{0,1,2:T(2,128)(2,1)}, u32[]{:S(2)}, u32[]{:S(2)}) collective-permute-start(bf16[128,1,128]{0,1,2:T(2,128)(2,1)S(1)} %get-tuple-element.48), channel_id=1, source_target_pairs={{4,0},{8,4},{12,8},{5,1},{9,5},{13,9},{6,2},{10,6},{14,10},{7,3},{... | collective-permute-start | bytes 98312 | tf_op jit(solution)/shard_map/ppermute | solution.py:23
  25.8 9.3 %copy-start.1 = (bf16[128,32,128]{2,1,0:T(8,128)(2,1)S(1)}, bf16[128,32,128]{2,1,0:T(8,128)(2,1)}, u32[]{:S(2)}) copy-start(bf16[128,32,128]{2,1,0:T(8,128)(2,1)} %param.5) | copy-start | bytes 3145732
  26.8 11.0 %collective-permute-start.2 = (bf16[128,34,1]{0,1,2:T(8,128)(2,1)}, bf16[128,34,1]{0,1,2:T(8,128)(2,1)}, u32[]{:S(2)}, u32[]{:S(2)}) collective-permute-start(bf16[128,34,1]{0,1,2:T(8,128)(2,1)} %get-tuple-element.37), channel_id=1, source_target_pairs={{0,1},{1,2},{2,3},{4,5},{5,6},{6,7},{8,9},{9,10},{10,11},{12,13},{... | collective-permute-start | bytes 26120 | tf_op jit(solution)/shard_map/ppermute | solution.py:21
  30.7 9.2 %collective-permute-start.3 = (bf16[128,34,1]{0,1,2:T(8,128)(2,1)}, bf16[128,34,1]{0,1,2:T(8,128)(2,1)}, u32[]{:S(2)}, u32[]{:S(2)}) collective-permute-start(bf16[128,34,1]{0,1,2:T(8,128)(2,1)} %get-tuple-element.38), channel_id=1, source_target_pairs={{1,0},{2,1},{3,2},{5,4},{6,5},{7,6},{9,8},{10,9},{11,10},{13,12},{... | collective-permute-start | bytes 26120 | tf_op jit(solution)/shard_map/ppermute | solution.py:23
  35.2 2.1 %copy-start.4 = (bf16[3,3,64,128]{3,2,1,0:T(8,128)(2,1)S(1)}, bf16[3,3,64,128]{3,2,1,0:T(8,128)(2,1)}, u32[]{:S(2)}) copy-start(bf16[3,3,64,128]{3,2,1,0:T(8,128)(2,1)} %param.7) | copy-start | bytes 442372
  44.3 1.6 copy-start.3
  58.5 18.8 %copy-start.5 = (s32[8,512]{1,0:T(8,128)S(1)}, s32[8,512]{1,0:T(8,128)}, u32[]{:S(2)}) copy-start(s32[8,512]{1,0:T(8,128)} %param.9) | copy-start | bytes 49156
  58.6 7.6 %collective-permute-start.10 = (f32[1,1,512]{2,1,0:T(1,128)S(1)}, f32[1,1,512]{2,1,0:T(1,128)S(1)}, u32[]{:S(2)}, u32[]{:S(2)}) collective-permute-start(f32[1,1,512]{2,1,0:T(1,128)S(1)} %get-tuple-element.89), channel_id=1, source_target_pairs={{0,1},{1,2},{2,3},{3,4},{4,5},{5,6},{6,7},{7,8},{8,9},{9,10},{10,1... | collective-permute-start | bytes 6152 | tf_op jit(solution)/shard_map/ppermute | solution.py:21
  60.0 6.2 %collective-permute-start.11 = (f32[1,1,512]{2,1,0:T(1,128)S(1)}, f32[1,1,512]{2,1,0:T(1,128)S(1)}, u32[]{:S(2)}, u32[]{:S(2)}) collective-permute-start(f32[1,1,512]{2,1,0:T(1,128)S(1)} %get-tuple-element.90), channel_id=1, source_target_pairs={{1,0},{2,1},{3,2},{4,3},{5,4},{6,5},{7,6},{8,7},{9,8},{10,9},{11,1... | collective-permute-start | bytes 6152 | tf_op jit(solution)/shard_map/ppermute | solution.py:23
  61.3 5.1 %collective-permute-start.8 = (f32[3,1,512]{2,1,0:T(1,128)S(1)}, f32[3,1,512]{2,1,0:T(1,128)S(1)}, u32[]{:S(2)}, u32[]{:S(2)}) collective-permute-start(f32[3,1,512]{2,1,0:T(1,128)S(1)} %get-tuple-element.71), channel_id=1, source_target_pairs={{0,1},{1,2},{2,3},{3,4},{4,5},{5,6},{6,7},{7,8},{8,9},{9,10},{10,1... | collective-permute-start | bytes 18440 | tf_op jit(solution)/shard_map/ppermute | solution.py:21
  64.8 4.3 %collective-permute-start.9 = (f32[3,1,512]{2,1,0:T(1,128)S(1)}, f32[3,1,512]{2,1,0:T(1,128)S(1)}, u32[]{:S(2)}, u32[]{:S(2)}) collective-permute-start(f32[3,1,512]{2,1,0:T(1,128)S(1)} %get-tuple-element.72), channel_id=1, source_target_pairs={{1,0},{2,1},{3,2},{4,3},{5,4},{6,5},{7,6},{8,7},{9,8},{10,9},{11,1... | collective-permute-start | bytes 18440 | tf_op jit(solution)/shard_map/ppermute | solution.py:23
  69.5 5.6 %collective-permute-start.12 = (f32[4,1,512]{2,1,0:T(1,128)S(1)}, f32[4,1,512]{2,1,0:T(1,128)S(1)}, u32[]{:S(2)}, u32[]{:S(2)}) collective-permute-start(f32[4,1,512]{2,1,0:T(1,128)S(1)} %get-tuple-element.69), channel_id=1, source_target_pairs={{0,1},{1,2},{2,3},{3,4},{4,5},{5,6},{6,7},{7,8},{8,9},{9,10},{10,1... | collective-permute-start | bytes 24584 | tf_op jit(solution)/shard_map/ppermute | solution.py:21
  73.8 3.3 %collective-permute-start.13 = (f32[4,1,512]{2,1,0:T(1,128)S(1)}, f32[4,1,512]{2,1,0:T(1,128)S(1)}, u32[]{:S(2)}, u32[]{:S(2)}) collective-permute-start(f32[4,1,512]{2,1,0:T(1,128)S(1)} %get-tuple-element.70), channel_id=1, source_target_pairs={{1,0},{2,1},{3,2},{4,3},{5,4},{6,5},{7,6},{8,7},{9,8},{10,9},{11,1... | collective-permute-start | bytes 24584 | tf_op jit(solution)/shard_map/ppermute | solution.py:23
  77.4 7.2 %collective-permute-start.14 = (f32[1,1,512]{2,1,0:T(1,128)S(1)}, f32[1,1,512]{2,1,0:T(1,128)S(1)}, u32[]{:S(2)}, u32[]{:S(2)}) collective-permute-start(f32[1,1,512]{2,1,0:T(1,128)S(1)} %get-tuple-element.87), channel_id=1, source_target_pairs={{0,1},{1,2},{2,3},{3,4},{4,5},{5,6},{6,7},{7,8},{8,9},{9,10},{10,1... | collective-permute-start | bytes 6152 | tf_op jit(solution)/shard_map/ppermute | solution.py:21
  83.3 3.1 %collective-permute-start.15 = (f32[1,1,512]{2,1,0:T(1,128)S(1)}, f32[1,1,512]{2,1,0:T(1,128)S(1)}, u32[]{:S(2)}, u32[]{:S(2)}) collective-permute-start(f32[1,1,512]{2,1,0:T(1,128)S(1)} %get-tuple-element.88), channel_id=1, source_target_pairs={{1,0},{2,1},{3,2},{4,3},{5,4},{6,5},{7,6},{8,7},{9,8},{10,9},{11,1... | collective-permute-start | bytes 6152 | tf_op jit(solution)/shard_map/ppermute | solution.py:23
  86.9 6.0 %collective-permute-start.16 = (f32[4,1,512]{2,1,0:T(1,128)S(1)}, f32[4,1,512]{2,1,0:T(1,128)S(1)}, u32[]{:S(2)}, u32[]{:S(2)}) collective-permute-start(f32[4,1,512]{2,1,0:T(1,128)S(1)} %get-tuple-element.67), channel_id=1, source_target_pairs={{0,1},{1,2},{2,3},{3,4},{4,5},{5,6},{6,7},{7,8},{8,9},{9,10},{10,1... | collective-permute-start | bytes 24584 | tf_op jit(solution)/shard_map/ppermute | solution.py:21
  91.6 3.1 %collective-permute-start.17 = (f32[4,1,512]{2,1,0:T(1,128)S(1)}, f32[4,1,512]{2,1,0:T(1,128)S(1)}, u32[]{:S(2)}, u32[]{:S(2)}) collective-permute-start(f32[4,1,512]{2,1,0:T(1,128)S(1)} %get-tuple-element.68), channel_id=1, source_target_pairs={{1,0},{2,1},{3,2},{4,3},{5,4},{6,5},{7,6},{8,7},{9,8},{10,9},{11,1... | collective-permute-start | bytes 24584 | tf_op jit(solution)/shard_map/ppermute | solution.py:23
  129.9 2.6 %collective-permute-start.18 = (f32[1,1,512]{2,1,0:T(1,128)S(1)}, f32[1,1,512]{2,1,0:T(1,128)S(1)}, u32[]{:S(2)}, u32[]{:S(2)}) collective-permute-start(f32[1,1,512]{2,1,0:T(1,128)S(1)} %get-tuple-element.85), channel_id=1, source_target_pairs={{0,1},{1,2},{2,3},{3,4},{4,5},{5,6},{6,7},{7,8},{8,9},{9,10},{10,1... | collective-permute-start | bytes 6152 | tf_op jit(solution)/shard_map/ppermute | solution.py:21
  131.2 3.1 %collective-permute-start.19 = (f32[1,1,512]{2,1,0:T(1,128)S(1)}, f32[1,1,512]{2,1,0:T(1,128)S(1)}, u32[]{:S(2)}, u32[]{:S(2)}) collective-permute-start(f32[1,1,512]{2,1,0:T(1,128)S(1)} %get-tuple-element.86), channel_id=1, source_target_pairs={{1,0},{2,1},{3,2},{4,3},{5,4},{6,5},{7,6},{8,7},{9,8},{10,9},{11,1... | collective-permute-start | bytes 6152 | tf_op jit(solution)/shard_map/ppermute | solution.py:23
  134.8 3.4 %collective-permute-start.20 = (f32[4,1,512]{2,1,0:T(1,128)S(1)}, f32[4,1,512]{2,1,0:T(1,128)S(1)}, u32[]{:S(2)}, u32[]{:S(2)}) collective-permute-start(f32[4,1,512]{2,1,0:T(1,128)S(1)} %get-tuple-element.65), channel_id=1, source_target_pairs={{0,1},{1,2},{2,3},{3,4},{4,5},{5,6},{6,7},{7,8},{8,9},{9,10},{10,1... | collective-permute-start | bytes 24584 | tf_op jit(solution)/shard_map/ppermute | solution.py:21
  136.9 3.1 %collective-permute-start.21 = (f32[4,1,512]{2,1,0:T(1,128)S(1)}, f32[4,1,512]{2,1,0:T(1,128)S(1)}, u32[]{:S(2)}, u32[]{:S(2)}) collective-permute-start(f32[4,1,512]{2,1,0:T(1,128)S(1)} %get-tuple-element.66), channel_id=1, source_target_pairs={{1,0},{2,1},{3,2},{4,3},{5,4},{6,5},{7,6},{8,7},{9,8},{10,9},{11,1... | collective-permute-start | bytes 24584 | tf_op jit(solution)/shard_map/ppermute | solution.py:23
where the time goes:
time: 179 us; the launch traced here: 178 us
  blocking collectives  77 us (43%)
  starting transfers between devices  51.5 us (29%)
  waiting for transfers between devices  17.9 us (10%)
  local copies, waits for them, and re-layouts  10.2 us (6%)
  other arithmetic  9.49 us (5%)
  between operations  6.62 us (4%)
  matrix products  5.29 us (3%)
    psum x2, blocking collectives, global_sums(): return lax.psum((values[0], values[1]), ('rows', 'cols', 'sub'))  65 us
    ppermute x11, starting transfers between devices, with_halo(): lax.ppermute(tail, axis, [(i, (i + 1) % count) for i in range(ends)])  37.3 us
    ppermute x11, waiting for transfers between devices, with_halo(): lax.ppermute(head, axis, [((i + 1) % count, i) for i in range(ends)])  17.8 us
    ppermute x11, starting transfers between devices, with_halo(): lax.ppermute(head, axis, [((i + 1) % count, i) for i in range(ends)])  14.2 us
    all_to_all x1, blocking collectives, on_device(): lax.all_to_all(stacked, ('cols', 'sub'), split_axis=1, concat_axis=2, til...  12 us
    concatenate x7, other arithmetic, with_halo(): jnp.concatenate([lax.ppermute(tail, axis, [(i, (i + 1) % count) for i in...  5.03 us
    dot_general x9, matrix products, head_maps(): jnp.dot(conv_weight[shift_r, shift_c], window_cell_count, preferred_eleme...  4.64 us
  transfers between devices with their start and end apart: 22, of which 8 were waited for; matrix products, arithmetic and copies ran while one was open for 6% of the time, Pallas kernels for 0%

commit v1 on v0

v1 whole, which is shorter than its diff:
```python
import functools

import jax
import jax.numpy as jnp
from jax import lax
from jax.experimental import pallas as pl
from jax.experimental.pallas import tpu as pltpu
from jax.sharding import PartitionSpec as P

RIDGE = 0.05
BASE_WEIGHT = 0.1
F32 = jnp.float32
BF16 = jnp.bfloat16
MESH = pl.DeviceIdType.MESH
DIRS = ((0, 1), (0, -1), (1, 0), (-1, 0), (1, 1), (1, -1), (-1, 1), (-1, -1))
SIDE = {1: 2, -1: 1, 0: 0}
HALO = 8


def box(x):
    v = x + pltpu.roll(x, 1, 0) + pltpu.roll(x, x.shape[0] - 1, 0)
    return v + pltpu.roll(v, 1, 1) + pltpu.roll(v, x.shape[1] - 1, 1)


def window_stats(g, inside9):
    avg = [box(c) * (1.0 / 9.0) for c in g]
    second = [box(g[i] * g[j]) * (1.0 / 9.0) for i, j in ((0, 0), (0, 1), (0, 2), (1, 1), (1, 2), (2, 2))]
    rr = second[0] - avg[0] * avg[0] + RIDGE
    rg = second[1] - avg[0] * avg[1]
    rb = second[2] - avg[0] * avg[2]
    gg = second[3] - avg[1] * avg[1] + RIDGE
    gb = second[4] - avg[1] * avg[2]
    bb = second[5] - avg[2] * avg[2] + RIDGE
    c_rr = gg * bb - gb * gb
    c_rg = rb * gb - rg * bb
    c_rb = rg * gb - rb * gg
    c_gg = rr * bb - rb * rb
    c_gb = rg * rb - rr * gb
    c_bb = rr * gg - rg * rg
    det = rr * c_rr + rg * c_rg + rb * c_rb
    scale = inside9 / det
    return avg, [c * scale for c in (c_rr, c_rg, c_rb, c_gg, c_gb, c_bb)]


def smooth(p, g, avg, inv, inside9):
    pb = box(p)
    x = [box(g[i] * p) - avg[i] * pb for i in range(3)]
    s0 = inv[0] * x[0] + inv[1] * x[1] + inv[2] * x[2]
    s1 = inv[1] * x[0] + inv[3] * x[1] + inv[4] * x[2]
    s2 = inv[2] * x[0] + inv[4] * x[1] + inv[5] * x[2]
    off = pb * inside9 - (s0 * avg[0] + s1 * avg[1] + s2 * avg[2])
    return box(s0) * g[0] + box(s1) * g[1] + box(s2) * g[2] + box(off)


def kernel(sizes, f_ref, g_ref, w_ref, hw_ref, m_ref, o_ref,
           wide, ft, edge, e_in, gbuf, sw, wmat, logit, mbuf, m_in, mtile, part, parts, obuf, o_in,
           f_send, f_recv, e_send, e_recv, g_send, g_recv, s_send, s_recv,
           m_send, m_recv, p_send, p_recv, o_send, o_recv):
    n_rows, n_cols, n_sub, chans, mids, th, tw, strip = sizes
    n_c = n_cols * n_sub
    n_all = n_rows * n_c
    row = lax.axis_index("rows")
    col = lax.axis_index("cols") * n_sub + lax.axis_index("sub")
    me = row * n_c + col

    def device(r, c):
        return {"rows": r, "cols": c // n_sub, "sub": c % n_sub}

    def exists(dy, dx):
        ok = None
        for pos, step, count in ((row, dy, n_rows), (col, dx, n_c)):
            if step:
                one = (pos + step < count) if step > 0 else (pos + step >= 0)
                ok = one if ok is None else jnp.logical_and(ok, one)
        return ok

    def neighbours(pick, make):
        def start():
            for d, (dy, dx) in enumerate(DIRS):
                if pick(dy, dx):
                    @pl.when(exists(dy, dx))
                    def _(d=d, dy=dy, dx=dx):
                        make(d, dy, dx, device(row + dy, col + dx)).start()

        def finish(sent):
            for d, (dy, dx) in enumerate(DIRS):
                if pick(dy, dx):
                    ey, ex = (dy, dx) if sent else (-dy, -dx)

                    @pl.when(exists(ey, ex))
                    def _(d=d, dy=dy, dx=dx):
                        copy = make(d, dy, dx, device(row + dy, col + dx))
                        if sent:
                            copy.wait_send()
                        else:
                            copy.wait_recv()

        return start, lambda: finish(False), lambda: finish(True)

    def field_copy(buf, send, recv):
        def make(d, dy, dx, dev):
            if dy == 0:
                src, dst = pl.ds(HALO, th), pl.ds(HALO, th)
            elif dy > 0:
                src, dst = pl.ds(th, HALO), pl.ds(0, HALO)
            else:
                src, dst = pl.ds(HALO, HALO), pl.ds(HALO + th, HALO)
            return pltpu.make_async_remote_copy(
                src_ref=buf.at[0, :, src, :], dst_ref=buf.at[SIDE[dx], :, dst, :],
                send_sem=send.at[d], recv_sem=recv.at[d], device_id=dev, device_id_type=MESH)
        return make

    def row_copy(d, dy, dx, dev):
        src, dst = (th * chans, 0) if dy > 0 else (chans, (th + 1) * chans)
        return pltpu.make_async_remote_copy(
            src_ref=ft.at[pl.ds(src, chans), :], dst_ref=ft.at[pl.ds(dst, chans), :],
            send_sem=f_send.at[d], recv_sem=f_recv.at[d], device_id=dev, device_id_type=MESH)

    def edge_copy(d, dy, dx, dev):
        return pltpu.make_async_remote_copy(
            src_ref=edge, dst_ref=e_in.at[d],
            send_sem=e_send.at[d], recv_sem=e_recv.at[d], device_id=dev, device_id_type=MESH)

    def across(src, dst, send, recv):
        def make(i):
            peer = lax.rem(col + i, n_c)
            return pltpu.make_async_remote_copy(
                src_ref=src.at[peer], dst_ref=dst.at[col],
                send_sem=send.at[i], recv_sem=recv.at[i],
                device_id=device(row, peer), device_id_type=MESH)
        return make

    def share(i):
        peer = lax.rem(me + i, n_all)
        return pltpu.make_async_remote_copy(
            src_ref=part, dst_ref=parts.at[me],
            send_sem=p_send.at[i], recv_sem=p_recv.at[i],
            device_id=device(peer // n_c, peer % n_c), device_id_type=MESH)

    gbuf[...] = jnp.zeros_like(gbuf)
    sw[...] = jnp.zeros_like(sw)
    e_in[...] = jnp.zeros_like(e_in)
    zero_row = jnp.zeros((chans, tw), BF16)
    ft[pl.ds(0, chans), :] = zero_row
    ft[pl.ds((th + 1) * chans, chans), :] = zero_row

    barrier = pltpu.get_barrier_semaphore()

    @pl.loop(1, n_all)
    def _(i):
        peer = lax.rem(me + i, n_all)
        pl.semaphore_signal(barrier, inc=1, device_id=device(peer // n_c, peer % n_c), device_id_type=MESH)

    for k in range(3):
        gbuf[0, k, pl.ds(HALO, th), :] = g_ref[k].astype(F32)
    for k in range(n_c):
        mbuf[k] = m_ref[:, k * tw:(k + 1) * tw].astype(F32)
    m_in[col] = mbuf[col]

    lane = lax.broadcasted_iota(jnp.int32, (chans, tw), 1)
    rows_at_once = 256

    @pl.loop(0, chans * th // rows_at_once)
    def _(i):
        at = pl.ds(pl.multiple_of(i * rows_at_once, rows_at_once), rows_at_once)
        wide[at, :] = f_ref[at, :].astype(F32)

    def one_row(y, acc):
        cells = wide[pl.ds(y, chans, stride=th), :]
        ft[pl.ds(pl.multiple_of((y + 1) * chans, chans), chans), :] = cells.astype(BF16)
        turned = pltpu.roll(cells, 2 * y + 2, 1)
        return jnp.where((lane == 2 * y + 1) | (lane == 2 * y + 2), turned, acc)

    edge[...] = lax.fori_loop(0, th, one_row, jnp.zeros((chans, tw), F32)).astype(BF16)

    pl.semaphore_wait(barrier, n_all - 1)

    rows_go, rows_come, rows_gone = neighbours(lambda dy, dx: dx == 0, row_copy)
    edge_go, edge_come, edge_gone = neighbours(lambda dy, dx: dx != 0, edge_copy)
    guide_go, guide_come, guide_gone = neighbours(lambda dy, dx: True, field_copy(gbuf, g_send, g_recv))
    sw_go, sw_come, sw_gone = neighbours(lambda dy, dx: True, field_copy(sw, s_send, s_recv))
    mask_copy = across(mbuf, m_in, m_send, m_recv)
    out_copy = across(obuf, o_in, o_send, o_recv)

    edge_go()
    rows_go()
    guide_go()
    for i in range(1, n_c):
        mask_copy(i).start()

    for v in range(3):
        for u in range(3):
            wmat[v * mids:(v + 1) * mids, u * chans:(u + 1) * chans] = w_ref[u, v]
    eye = lax.broadcasted_iota(jnp.int32, (mids, mids), 0) == lax.broadcasted_iota(jnp.int32, (mids, mids), 1)
    head = [
        jnp.broadcast_to(
            jnp.sum(jnp.where(eye, jnp.broadcast_to(hw_ref[k:k + 1, :], (mids, mids)), 0.0), axis=1, keepdims=True),
            (mids, tw))
        for k in range(2)
    ]

    edge_come()
    odd = lane % 2 == 1

    def sides(dy):
        from_left = e_in[DIRS.index((dy, 1))].astype(F32)
        from_right = e_in[DIRS.index((dy, -1))].astype(F32)
        return jnp.where(odd, from_left, from_right)

    rim = jnp.where((lane >= 1) & (lane <= 2 * th), sides(0), 0.0)
    rim = jnp.where((lane == tw - 1) | (lane == 0), pltpu.roll(sides(1), tw - 2 * th, 1), rim)
    rim = jnp.where((lane == 2 * th + 1) | (lane == 2 * th + 2), pltpu.roll(sides(-1), 2 * th, 1), rim)
    rim3 = jnp.concatenate([pltpu.roll(rim, 2, 1), rim, pltpu.roll(rim, tw - 2, 1)], axis=0).astype(BF16)
    from_left = jnp.dot(wmat[0:mids, :], rim3, preferred_element_type=F32)
    from_right = jnp.dot(wmat[2 * mids:3 * mids, :], rim3, preferred_element_type=F32)
    rim_sum = jnp.where(odd[:mids], pltpu.roll(from_left, 2, 1), from_right)
    lane_m = lane[:mids]

    rows_come()

    @pl.loop(0, th // 2)
    def _(t):
        y0 = t * 2
        rhs = jnp.concatenate(
            [ft[pl.ds(pl.multiple_of((y0 + j) * chans, chans), 3 * chans), :] for j in range(2)], axis=1)
        prod = jnp.dot(wmat[...], rhs, preferred_element_type=F32)
        for j in range(2):
            y = y0 + j
            p = prod[:, j * tw:(j + 1) * tw]
            here = pltpu.roll(rim_sum, lax.rem(2 * tw - (2 * y + 3), tw), 1)
            conv = (p[mids:2 * mids]
                    + jnp.where(lane_m == 0, here, pltpu.roll(p[:mids], 1, 1))
                    + jnp.where(lane_m == tw - 1, here, pltpu.roll(p[2 * mids:], tw - 1, 1)))
            hidden = jnp.maximum(conv, 0.0)
            for k in range(2):
                logit[k, pl.ds(y, 1), :] = jnp.sum(hidden * head[k], axis=0, keepdims=True)

    for i in range(1, n_c):
        mask_copy(i).wait_recv()
    for k in range(n_c):
        mtile[k * strip:(k + 1) * strip, :] = m_in[k]

    seed = 1.0 / (1.0 + jnp.exp(-logit[0]))
    raw = logit[1]
    confidence = jnp.maximum(raw, 0.0) + jnp.log(1.0 + jnp.exp(-jnp.abs(raw)))
    sw[0, 0, pl.ds(HALO, th), :] = seed
    sw[0, 1, pl.ds(HALO, th), :] = BASE_WEIGHT + mtile[...] * confidence
    sw_go()

    ext_h = th + 2 * HALO
    lane_e = lax.broadcasted_iota(jnp.int32, (ext_h, tw), 1)

    def extended(buf, k):
        return jnp.concatenate([buf[0, k], jnp.where(lane_e < tw // 2, buf[1, k], buf[2, k])], axis=1)

    at_row = lax.broadcasted_iota(jnp.int32, (ext_h, 2 * tw), 0) + (row * th - HALO)
    at_col = lax.broadcasted_iota(jnp.int32, (ext_h, 2 * tw), 1)
    at_col = jnp.where(at_col >= tw + tw // 2, at_col - 2 * tw, at_col) + col * tw
    inside = (at_row >= 0) & (at_row < n_rows * th) & (at_col >= 0) & (at_col < n_c * tw)
    inside9 = jnp.where(inside, 1.0 / 9.0, 0.0)

    guide_come()
    g = [extended(gbuf, k) for k in range(3)]
    avg, inv = window_stats(g, inside9)

    sw_come()
    s = extended(sw, 0)
    w = extended(sw, 1)
    r = jnp.where(inside, smooth(s, g, avg, inv, inside9) - 9.0 * s, 0.0)
    q = jnp.where(inside, (9.0 + w) * r - smooth(r, g, avg, inv, inside9), 0.0)
    aq = (9.0 + w) * q - smooth(q, g, avg, inv, inside9)

    def core(x):
        return x[HALO:HALO + th, :tw]

    r, q, aq = core(r), core(q), core(aq)
    part[...] = jnp.zeros_like(part)
    for k, x in enumerate((r * r, r * q, q * q, q * aq)):
        part[k:k + 1, :] = jnp.sum(x, axis=0, keepdims=True)
    parts[me] = part[...]

    @pl.loop(1, n_all)
    def _(i):
        share(i).start()

    @pl.loop(1, n_all)
    def _(i):
        share(i).wait_recv()

    total = jnp.sum(jnp.sum(parts[...], axis=0), axis=1, keepdims=True)
    rr, rq, qq, qaq = (total[k:k + 1, :] for k in range(4))
    a0 = rr / rq
    rr1 = a0 * a0 * qq - rr
    b1 = 1.0 + rr1 / rr
    a1 = rr1 / (b1 * b1 * rq - 2.0 * a0 * b1 * qq + a0 * a0 * qaq)
    mixture = core(s) + (a0 + a1 * b1) * r - (a0 * a1) * q

    for k in range(n_c):
        obuf[k] = mixture[k * strip:(k + 1) * strip, :]
    o_in[col] = obuf[col]
    for i in range(1, n_c):
        out_copy(i).start()

    edge_gone()
    rows_gone()
    guide_gone()
    sw_gone()

    @pl.loop(1, n_all)
    def _(i):
        share(i).wait_send()

    for i in range(1, n_c):
        mask_copy(i).wait_send()
        out_copy(i).wait_recv()
    for k in range(n_c):
        o_ref[:, k * tw:(k + 1) * tw] = o_in[k]
    for i in range(1, n_c):
        out_copy(i).wait_send()


def on_device(mesh, features, guide_image, conv_weight, head_weight, pixel_mask):
    chans, th, tw = features.shape
    mids = conv_weight.shape[2]
    strip = pixel_mask.shape[0]
    n_rows, n_cols, n_sub = (mesh.shape[a] for a in ("rows", "cols", "sub"))
    n_c = n_cols * n_sub
    n_all = n_rows * n_c
    sizes = (n_rows, n_cols, n_sub, chans, mids, th, tw, strip)
    dma = pltpu.SemaphoreType.DMA
    vmem = pl.BlockSpec(memory_space=pltpu.VMEM)
    ext_h = th + 2 * HALO
    return pl.pallas_call(
        functools.partial(kernel, sizes),
        out_shape=jax.ShapeDtypeStruct((strip, n_c * tw), F32),
        in_specs=[vmem] * 5,
        out_specs=vmem,
        scratch_shapes=[
            pltpu.VMEM((chans * th, tw), F32),
            pltpu.VMEM(((th + 2) * chans, tw), BF16),
            pltpu.VMEM((chans, tw), BF16),
            pltpu.VMEM((8, chans, tw), BF16),
            pltpu.VMEM((3, 3, ext_h, tw), F32),
            pltpu.VMEM((3, 2, ext_h, tw), F32),
            pltpu.VMEM((3 * mids, 3 * chans), BF16),
            pltpu.VMEM((2, th, tw), F32),
            pltpu.VMEM((n_c, strip, tw), F32),
            pltpu.VMEM((n_c, strip, tw), F32),
            pltpu.VMEM((th, tw), F32),
            pltpu.VMEM((8, tw), F32),
            pltpu.VMEM((n_all, 8, tw), F32),
            pltpu.VMEM((n_c, strip, tw), F32),
            pltpu.VMEM((n_c, strip, tw), F32),
            dma((8,)), dma((8,)), dma((8,)), dma((8,)), dma((8,)), dma((8,)), dma((8,)), dma((8,)),
            dma((n_c,)), dma((n_c,)), dma((n_all,)), dma((n_all,)), dma((n_c,)), dma((n_c,)),
        ],
        compiler_params=pltpu.CompilerParams(
            collective_id=0, has_side_effects=True, vmem_limit_bytes=40 * 1024 * 1024),
    )(features.reshape(chans * th, tw), guide_image, conv_weight, head_weight, pixel_mask)


def solution(mesh):
    return jax.shard_map(
        functools.partial(on_device, mesh),
        mesh=mesh,
        in_specs=(
            P(None, ("groups", "rows"), ("cols", "sub")),
            P(None, ("groups", "rows"), ("cols", "sub")),
            P(),
            P(),
            P(("groups", "rows", "cols", "sub"), None),
        ),
        out_specs=P(("groups", "rows", "cols", "sub"), None),
        check_vma=False,
    )
```

time: 179 us -> 34.2 us (0.19)
  blocking collectives: 77 us -> 0 us
  starting transfers between devices: 51.5 us -> 0 us
  Pallas kernels: 0 us -> 29 us
  waiting for transfers between devices: 17.9 us -> 0 us
  other arithmetic: 9.49 us -> 0 us
  between operations: 6.62 us -> 0.01 us
  local copies, waits for them, and re-layouts: 10.2 us -> 4.87 us
  matrix products: 5.29 us -> 0 us
    psum x2 -> x0, blocking collectives: 65 us -> none  [global_sums(): return lax.psum((values[0], values[1]), ('rows', 'cols', 'sub'))]
    ppermute x22 -> x0, starting transfers between devices: 51.5 us -> none  [the longest x11 37.3 us: with_halo(): lax.ppermute(tail, axis, [(i, (i + 1) % count) for i in range(ends)])]
    pallas_call x0 -> x1, Pallas kernels: none -> 29 us  [on_device(): pl.pallas_call(functools.partial(kernel, sizes), out_shape=jax.ShapeDtype...]
    ppermute x22 -> x0, waiting for transfers between devices: 17.9 us -> none  [the longest x11 17.8 us: with_halo(): lax.ppermute(head, axis, [((i + 1) % count, i) for i in range(ends)])]
    all_to_all x1 -> x0, blocking collectives: 12 us -> none  [on_device(): lax.all_to_all(stacked, ('cols', 'sub'), split_axis=1, concat_axis=2, til...]
    dot_general x10 -> x0, matrix products: 5.29 us -> none  [the longest x9 4.64 us: head_maps(): jnp.dot(conv_weight[shift_r, shift_c], window_cell_count, preferred_eleme...]
    concatenate x8 -> x0, other arithmetic: 5.05 us -> none  [the longest x7 5.03 us: with_halo(): jnp.concatenate([lax.ppermute(tail, axis, [(i, (i + 1) % count) for i in...]
    ppermute x3 -> x0, local copies, waits for them, and re-layouts: 3.9 us -> none  [the longest x2 2.31 us: with_halo(): lax.ppermute(tail, axis, [(i, (i + 1) % count) for i in range(ends)])]
  transfers between devices with their start and end apart: 22 -> 0, of which waited for: 8 -> 0; matrix products, arithmetic and copies ran while one was open for 6% -> 0% of each run, Pallas kernels for 0% -> 0%
where the time goes in v1:
time: 34.2 us; the launch traced here: 33.9 us
  Pallas kernels  29 us (85%)
  local copies, waits for them, and re-layouts  4.87 us (14%)
    pallas_call x1, Pallas kernels, on_device(): pl.pallas_call(functools.partial(kernel, sizes), out_shape=jax.ShapeDtype...  29 us
    unnamed x11, local copies, waits for them, and re-layouts  4.87 us

profile of v1, /device:TPU:0, one launch (start us, length us, event | category | flops | bytes accessed | tf_op | source)
XLA Modules:
  0.0 33.9 jit_solution(219399443324444868)
XLA Ops:
  0.0 0.0 copy-start.4
  0.0 0.7 %copy-done.4 = f32[2,64]{1,0:T(2,128)S(1)} copy-done((f32[2,64]{1,0:T(2,128)S(1)}, f32[2,64]{1,0:T(2,128)}, u32[]{:S(2)}) %copy-start.4) | copy-done | bytes 536
  0.7 0.0 copy-start
  0.7 1.2 %copy-done = bf16[128,32,128]{2,1,0:T(8,128)(2,1)S(1)} copy-done((bf16[128,32,128]{2,1,0:T(8,128)(2,1)S(1)}, bf16[128,32,128]{2,1,0:T(8,128)(2,1)}, u32[]{:S(2)}) %copy-start) | copy-done | bytes 1048600
  1.9 0.0 copy-start.1
  1.9 0.9 %copy-done.1 = bf16[3,3,64,128]{3,2,1,0:T(8,128)(2,1)S(1)} copy-done((bf16[3,3,64,128]{3,2,1,0:T(8,128)(2,1)S(1)}, bf16[3,3,64,128]{3,2,1,0:T(8,128)(2,1)}, u32[]{:S(2)}) %copy-start.1) | copy-done | bytes 147480
  2.8 0.0 copy-start.2
  2.8 0.7 %copy-done.2 = bf16[3,32,128]{2,1,0:T(8,128)(2,1)S(1)} copy-done((bf16[3,32,128]{2,1,0:T(8,128)(2,1)S(1)}, bf16[3,32,128]{2,1,0:T(8,128)(2,1)}, u32[]{:S(2)}) %copy-start.2) | copy-done | bytes 24600
  3.6 0.0 copy-start.3
  3.6 0.7 %copy-done.3 = s32[8,512]{1,0:T(8,128)S(1)} copy-done((s32[8,512]{1,0:T(8,128)S(1)}, s32[8,512]{1,0:T(8,128)}, u32[]{:S(2)}) %copy-start.3) | copy-done | bytes 16408
  4.3 29.0 %shard_map.55 = f32[8,512]{1,0:T(8,128)S(1)} custom-call(bf16[4096,128]{1,0:T(8,128)(2,1)S(1)} %bitcast.1, bf16[3,32,128]{2,1,0:T(8,128)(2,1)S(1)} %copy-done.2, bf16[3,3,64,128]{3,2,1,0:T(8,128)(2,1)S(1)} %copy-done.1, f32[2,64]{1,0:T(2,128)S(1)} %copy-done.4, s32[8,512]{1,0:T(8,128)S(1)} %copy-done.3), custom_call_target="tpu_custom_call" | custom-call | tf_op jit(solution)/shard_map/pallas_call | solution.py:333
  33.3 0.6 %copy.7 = f32[8,512]{1,0:T(8,128)} copy(f32[8,512]{1,0:T(8,128)S(1)} %shard_map.55) | data formatting | bytes 32768
Async XLA Ops:
  0.0 0.7 %copy-start.4 = (f32[2,64]{1,0:T(2,128)S(1)}, f32[2,64]{1,0:T(2,128)}, u32[]{:S(2)}) copy-start(f32[2,64]{1,0:T(2,128)} %hw_ref.1) | copy-start | bytes 1540
  0.7 1.2 %copy-start = (bf16[128,32,128]{2,1,0:T(8,128)(2,1)S(1)}, bf16[128,32,128]{2,1,0:T(8,128)(2,1)}, u32[]{:S(2)}) copy-start(bf16[128,32,128]{2,1,0:T(8,128)(2,1)} %param.5) | copy-start | bytes 3145732
  1.9 0.9 %copy-start.1 = (bf16[3,3,64,128]{3,2,1,0:T(8,128)(2,1)S(1)}, bf16[3,3,64,128]{3,2,1,0:T(8,128)(2,1)}, u32[]{:S(2)}) copy-start(bf16[3,3,64,128]{3,2,1,0:T(8,128)(2,1)} %w_ref.1) | copy-start | bytes 442372
  2.8 0.7 %copy-start.2 = (bf16[3,32,128]{2,1,0:T(8,128)(2,1)S(1)}, bf16[3,32,128]{2,1,0:T(8,128)(2,1)}, u32[]{:S(2)}) copy-start(bf16[3,32,128]{2,1,0:T(8,128)(2,1)} %g_ref.1) | copy-start | bytes 73732
  3.6 0.7 %copy-start.3 = (s32[8,512]{1,0:T(8,128)S(1)}, s32[8,512]{1,0:T(8,128)}, u32[]{:S(2)}) copy-start(s32[8,512]{1,0:T(8,128)} %m_ref.1) | copy-start | bytes 49156
